TPU v7x, 256 devices: a whole 4x4x8 slice. The times are simulated.
256 devices in a mesh: seq: 32 (over z, y), mp: 4 (over x), req: 2 (over core).
Axes of the slice: x: 4, y: 4, z: 8, core: 2. Of those that a mesh axis runs over, the one named last changes fastest.
Arguments:
- hidden: bfloat16 [2, 8192, 3072], P('req', 'seq', 'mp'), may hold values from -6 to 6
- norm_gain: bfloat16 [3072], replicated, may hold values from 0.5 to 1.5
- w_query: bfloat16 [3072, 1024], P(None, 'mp'), may hold values from -0.109375 to 0.109375
- w_keyval: bfloat16 [3072, 512], P(None, 'mp'), may hold values from -0.109375 to 0.109375
- w_attn_out: bfloat16 [1024, 3072], P('mp'), may hold values from -1.5 to 1.5
- w_inner: bfloat16 [3072, 2, 1536], P(None, None, 'mp'), may hold values from -0.109375 to 0.109375
- w_bc: bfloat16 [3072, 512], P(None, 'mp'), may hold values from -0.109375 to 0.109375
- w_dt: bfloat16 [3072, 12], P(None, 'mp'), may hold values from -0.109375 to 0.109375
- dt_bias: float32 [12], P('mp'), may hold values from -4 to 0
- a_log: float32 [12], P('mp'), may hold values from -12 to 0
- d_skip: float32 [12], P('mp'), may hold values from 0.1 to 10
- conv_x: bfloat16 [4, 1536], P(None, 'mp'), may hold values from -3 to 3
- conv_bc: bfloat16 [4, 512], replicated, may hold values from -3 to 3
- mamba_gain: bfloat16 [1536], P('mp'), may hold values from 0.5 to 1.5
- w_mamba_out: bfloat16 [1536, 3072], P('mp'), may hold values from -0.15625 to 0.15625
- cache: bfloat16 [2, 8192, 512], P('req', 'seq', 'mp'), may hold values from -70 to 70, as said below
- cache_len: int32 [2], P('req'), may hold values from 256 to 8192
- tail_x: bfloat16 [2, 3, 1536], P('req', None, 'mp'), may hold values from -6 to 6
- tail_bc: bfloat16 [2, 3, 512], P('req'), may hold values from -6 to 6
- ssm_init: float32 [2, 12, 128, 256], P('req', 'mp'), may hold values from -6 to 6
Outputs:
- layer_out: bfloat16 [2, 8192, 3072], P('req', 'seq', 'mp')
- new_keyval: bfloat16 [2, 8192, 512], P('req', 'seq', 'mp')
- block_states: float32 [2, 32, 12, 128, 256], P('req', 'seq', 'mp')
Inputs may be any that keep to these rules, and one draw needn't show every extreme that they name: Rows of the cache at or past cache_len are unused.
All inputs are finite; a program needn't handle non-finite values.
Results may differ from a plain program's by a relative error of at most 0.0097.
Values may be sent and summed in bfloat16 or wider, within the bound.
A program may use at most 192 MiB of HBM per device.

v0:
```python
import jax
import jax.numpy as jnp
from jax import lax
from jax.sharding import PartitionSpec as P

HD = 128
QH = 8
KVH = 2
NS = 256
CONV = 4
epsilon = 1e-05
rope_base = 100000000000.0
negative = -1e30


def shifted(block, axis, distance):
    devices = range(lax.axis_size(axis))
    route = [(i - distance, i) for i in devices if i - distance in devices]
    return lax.ppermute(block, axis, route)


def prefix(part, axis, combine, identity):
    place = lax.axis_index(axis)
    gathered = jax.tree.map(lambda a: lax.all_gather(a, axis), part)
    state = jax.tree.map(lambda a, e: jnp.zeros_like(a) + jnp.asarray(e, a.dtype), part, identity)

    def one(turn, state):
        return combine(
            state, jax.tree.map(lambda a: lax.dynamic_index_in_dim(a, turn, 0, False), gathered)
        )

    return lax.fori_loop(0, place, one, state)


def rotate(values, positions):
    half = HD // 2
    freqs = rope_base ** (-jnp.arange(half, dtype=jnp.float32) * 2.0 / HD)
    angles = positions.astype(jnp.float32)[:, None] * freqs[None, :]
    cosine = jnp.cos(angles)[:, None, :]
    sine = jnp.sin(angles)[:, None, :]
    first = values[..., :half]
    second = values[..., half:]
    return jnp.concatenate(
        [first * cosine - second * sine, second * cosine + first * sine], axis=-1
    )


def rms_scale(values):
    mean_sq = jnp.mean(values * values, axis=-1, keepdims=True)
    return values * lax.rsqrt(mean_sq + epsilon)


def causal_conv(tail, inputs, taps):
    padded = jnp.concatenate([tail, inputs], axis=0).astype(jnp.float32)
    count = inputs.shape[0]
    total = jnp.zeros(inputs.shape, jnp.float32)
    for offset in range(CONV):
        total = total + taps[offset].astype(jnp.float32)[None, :] * padded[offset : offset + count]
    return jax.nn.silu(total)


def join_states(earlier, later):
    return (earlier[0] * later[0], later[0][:, None, None] * earlier[1] + later[1])


def shards(
    hidden,
    norm_gain,
    w_query,
    w_keyval,
    w_attn_out,
    w_inner,
    w_bc,
    w_dt,
    dt_bias,
    a_log,
    d_skip,
    conv_x,
    conv_bc,
    mamba_gain,
    w_mamba_out,
    cache,
    cache_len,
    tail_x,
    tail_bc,
    ssm_init,
):
    high = lax.Precision.HIGHEST
    own_rows = hidden[0]
    tokens = own_rows.shape[0]
    seq_pos = lax.axis_index("seq")
    mp_pos = lax.axis_index("mp")
    length = cache_len[0]
    whole = lax.all_gather(own_rows, "mp", axis=1, tiled=True)
    normed = (rms_scale(whole.astype(jnp.float32)) * norm_gain.astype(jnp.float32)).astype(
        jnp.bfloat16
    )
    positions = length + seq_pos * tokens + jnp.arange(tokens, dtype=jnp.int32)
    local_heads = w_query.shape[1] // HD
    query = rotate(
        jnp.dot(normed, w_query, preferred_element_type=jnp.float32).reshape(
            tokens, local_heads, HD
        ),
        positions,
    ).astype(jnp.bfloat16)
    projected = jnp.dot(normed, w_keyval, preferred_element_type=jnp.float32)
    roped = rotate(projected[:, None, :], positions)[:, 0, :]
    kv_block = jnp.where(mp_pos % 2 == 0, roped, projected).astype(jnp.bfloat16)
    bc_block = jnp.dot(normed, w_bc, preferred_element_type=jnp.float32).astype(jnp.bfloat16)
    bc_all = lax.all_gather(bc_block, "mp", axis=1, tiled=True)
    own_rows_kv = jnp.concatenate([cache[0], kv_block], axis=0)
    mp_size = lax.axis_size("mp")
    partner = lax.ppermute(own_rows_kv, "mp", [(i, i ^ 1) for i in range(mp_size)])
    is_key_block = mp_pos % 2 == 0
    group_rows = jnp.where(
        is_key_block,
        jnp.concatenate([own_rows_kv, partner], axis=1),
        jnp.concatenate([partner, own_rows_kv], axis=1),
    )
    inner = jnp.einsum("td,dkc->tkc", normed, w_inner, preferred_element_type=jnp.float32).astype(
        jnp.bfloat16
    )
    rim = CONV - 1
    prev_x, prev_bc = shifted((inner[tokens - rim :, 1], bc_all[tokens - rim :]), "seq", 1)
    first_block = seq_pos == 0
    prev_x = jnp.where(first_block, tail_x[0], prev_x)
    prev_bc = jnp.where(first_block, tail_bc[0], prev_bc)
    mamba_heads = dt_bias.shape[0]
    x_conv = causal_conv(prev_x, inner[:, 1], conv_x).reshape(tokens, mamba_heads, HD)
    bc_conv = causal_conv(prev_bc, bc_all, conv_bc)
    b_mat = bc_conv[:, :NS]
    c_mat = bc_conv[:, NS:]
    step_size = jax.nn.softplus(jnp.dot(normed, w_dt, preferred_element_type=jnp.float32) + dt_bias)
    log_decay = -step_size * jnp.exp(a_log)[None, :]
    cumulative = jnp.cumsum(log_decay, axis=0)
    pairs = jnp.dot(c_mat, b_mat.T, precision=high)
    gap = cumulative[:, None, :] - cumulative[None, :, :]
    token_ids = jnp.arange(tokens)
    lower = (token_ids[:, None] >= token_ids[None, :])[:, :, None]
    decay = jnp.where(lower, jnp.exp(jnp.where(lower, gap, 0.0)), 0.0)
    mixing = decay * pairs[:, :, None] * step_size[None, :, :]
    inner_out = jnp.einsum("tsh,shp->thp", mixing, x_conv, precision=high)
    to_end = jnp.exp(cumulative[-1][None, :] - cumulative) * step_size
    own_state = jnp.einsum("sh,shp,sn->hpn", to_end, x_conv, b_mat, precision=high)
    block_decay = jnp.exp(cumulative[-1])
    seq_size = lax.axis_size("seq")
    rows = HD // seq_size
    pieces = jnp.transpose(own_state.reshape(mamba_heads, seq_size, rows, NS), (1, 0, 2, 3))
    decays = jnp.broadcast_to(block_decay[None, :, None, None], (seq_size, mamba_heads, 1, NS))
    columns = lax.all_to_all(jnp.concatenate([pieces, decays], axis=2), "seq", 0, 0, tiled=True)
    carry = lax.dynamic_slice_in_dim(ssm_init[0], seq_pos * rows, rows, 1)
    entering = []
    for source in range(seq_size):
        entering.append(carry)
        part = columns[source]
        carry = part[:, rows:, :] * carry + part[:, :rows, :]
    entering = lax.all_to_all(jnp.stack(entering, axis=0), "seq", 0, 0, tiled=True)
    incoming = jnp.transpose(entering, (1, 0, 2, 3)).reshape(mamba_heads, HD, NS)
    carried = jnp.exp(cumulative)[:, :, None] * jnp.einsum(
        "tn,hpn->thp", c_mat, incoming, precision=high
    )
    mamba_y = inner_out + carried + d_skip[None, :, None] * x_conv
    state_after = block_decay[:, None, None] * incoming + own_state
    gated = mamba_y * jax.nn.silu(inner[:, 0].astype(jnp.float32).reshape(tokens, mamba_heads, HD))
    mixed = (
        rms_scale(gated).reshape(tokens, mamba_heads * HD) * mamba_gain.astype(jnp.float32)
    ).astype(jnp.bfloat16)
    cache_rows = cache.shape[1]
    shard_rows = cache_rows + tokens
    group = mp_pos * local_heads // (QH // KVH)
    query_index = seq_pos * tokens + jnp.arange(tokens, dtype=jnp.int32)
    scale = 1.0 / float(HD) ** 0.5
    piece = lax.all_gather(group_rows, "seq", axis=0, tiled=True)
    top = jnp.full((local_heads, tokens), negative, jnp.float32)
    count = piece.shape[0]
    index = jnp.arange(count, dtype=jnp.int32)
    owner = index // shard_rows
    offset = index % shard_rows
    in_cache = offset < cache_rows
    slot_ok = in_cache & (owner * cache_rows + offset < length)
    new_index = owner * tokens + offset - cache_rows
    valid = slot_ok[None, :] | (~in_cache)[None, :] & (new_index[None, :] <= query_index[:, None])
    scores = (
        jnp.einsum("qhd,kd->hqk", query, piece[:, :HD], preferred_element_type=jnp.float32) * scale
    )
    masked = jnp.where(valid[None], scores, negative)
    new_top = jnp.maximum(top, jnp.max(masked, axis=-1))
    weights = jnp.where(valid[None], jnp.exp(masked - new_top[:, :, None]), 0.0)
    total = jnp.sum(weights, axis=-1)
    accum = jnp.einsum(
        "hqk,kd->hqd",
        weights.astype(jnp.bfloat16),
        piece[:, HD : 2 * HD],
        preferred_element_type=jnp.float32,
    )
    top, total, accum = (new_top, total, accum)
    attended = jnp.transpose(accum / total[:, :, None], (1, 0, 2)).reshape(tokens, local_heads * HD)
    attended = attended.astype(jnp.bfloat16)
    term = jnp.dot(attended, w_attn_out, preferred_element_type=jnp.float32)
    term = term + jnp.dot(mixed, w_mamba_out, preferred_element_type=jnp.float32)
    summed = lax.psum_scatter(term, "mp", scatter_dimension=1, tiled=True)
    layer = (summed + own_rows.astype(jnp.float32)).astype(jnp.bfloat16)
    return (layer[None], kv_block[None], state_after[None, None])


def solution(mesh):
    placed = (
        P("req", "seq", "mp"),
        P(),
        P(None, "mp"),
        P(None, "mp"),
        P("mp", None),
        P(None, None, "mp"),
        P(None, "mp"),
        P(None, "mp"),
        P("mp"),
        P("mp"),
        P("mp"),
        P(None, "mp"),
        P(),
        P("mp"),
        P("mp", None),
        P("req", "seq", "mp"),
        P("req"),
        P("req", None, "mp"),
        P("req", None, None),
        P("req", "mp", None, None),
    )
    return jax.shard_map(
        shards,
        mesh=mesh,
        in_specs=placed,
        out_specs=(P("req", "seq", "mp"), P("req", "seq", "mp"), P("req", "seq", "mp", None, None)),
        check_vma=False,
    )
```

profile of v0, /device:TPU:1, one launch (start us, length us, event | category | flops | bytes accessed | tf_op | source)
XLA Modules:
  0.0 306.3 jit_solution(14901815859498077116)
XLA Ops:
  9.9 0.9 copy.66
  11.5 1.5 convert_reduce_fusion.3
  13.0 1.4 slice_convert_fusion.4
  15.7 27.0 %all-gather.6.cloned.1.call-done = bf16[1,256,3072]{2,1,0:T(8,128)(2,1)} async-done(((bf16[1,256,768]{2,1,0:T(8,128)(2,1)}), bf16[1,256,3072]{2,1,0:T(8,128)(2,1)}) %all-gather.6.cloned.1.call-update) | async-done | bytes 1572880 | tf_op jit(solution)/shard_map/all_gather | solution.py:94
  42.7 1.9 fusion.9
  44.7 1.9 fusion.11
  46.6 1.4 fusion.13
  48.7 0.8 slice_convert_fusion
  50.0 0.9 reduce-window.6
  52.8 2.2 convolution_convert_fusion
  55.0 2.1 fusion.98
  58.3 3.1 %collective-permute-start.1 = (bf16[3,384]{1,0:T(4,128)(2,1)S(1)}, bf16[3,384]{1,0:T(4,128)(2,1)S(1)}, u32[]{:S(2)}, u32[]{:S(2)}) collective-permute-start(bf16[3,384]{1,0:T(4,128)(2,1)S(1)} %copy-done.18), channel_id=1, source_target_pairs={{0,8},{8,16},{16,24},{24,32},{32,40},{40,48},{48,56},{56,64},{64,7... | collective-permute-start | bytes 6920 | tf_op jit(solution)/shard_map/ppermute | solution.py:19
  61.4 9.7 %all_gather.11 = bf16[256,512]{1,0:T(8,128)(2,1)S(1)} all-gather(bf16[256,128]{1,0:T(8,128)(2,1)S(1)} %convolution_convert_fusion), channel_id=1, replica_groups=mesh['seq'=32,'mp'=4,'req'=2] {'mp'}, dimensions={1}, use_global_device_ids=true | all-gather | bytes 327680 | tf_op jit(solution)/shard_map/all_gather | solution.py:110
  71.1 3.1 %collective-permute-start.2 = (bf16[3,512]{1,0:T(4,128)(2,1)S(1)}, bf16[3,512]{1,0:T(4,128)(2,1)S(1)}, u32[]{:S(2)}, u32[]{:S(2)}) collective-permute-start(bf16[3,512]{1,0:T(4,128)(2,1)S(1)} %slice.510), channel_id=1, source_target_pairs={{0,8},{8,16},{16,24},{24,32},{32,40},{40,48},{48,56},{56,64},{64,7... | collective-permute-start | bytes 9224 | tf_op jit(solution)/shard_map/ppermute | solution.py:19
  75.0 0.9 divide_multiply_fusion.1
  75.9 0.9 copy.72
  76.8 0.7 bitcast_select_fusion.1
  78.1 1.5 fusion.45
  79.9 1.0 pad_maximum_fusion
  80.9 9.3 %all-to-all-start = ((f32[32,3,5,256]{3,1,2,0:T(4,128)}), f32[32,3,5,256]{3,1,2,0:T(4,128)}, u32[]{:S(2)}, u32[]{:S(2)}) async-start(f32[32,3,5,256]{3,1,2,0:T(4,128)} %pad_maximum_fusion), calls=%async_computation | async-start | bytes 1310720 | tf_op jit(solution)/shard_map/all_to_all | solution.py:150
  90.3 1.8 maximum_select_fusion
  92.1 15.6 %and_or_fusion = pred[256,16384]{0,1:T(8,128)(4,1)} fusion(s32[256]{0:T(256)S(1)} %copy-done.22, s32[16384]{0:T(1024)S(1)} %copy-done.6, pred[16384]{0:T(1024)(128)(4,1)S(1)} %copy-done.7, pred[16384]{0:T(1024)(128)(4,1)S(1)} %get-tuple-element.103), kind=kLoop, calls=%fused_computation.7 | loop fusion | flops 12582912 | bytes 4293632 | tf_op jit(solution)/shard_map/or | solution.py:182
  107.7 0.7 constant_dynamic-slice_fusion
  109.1 1.9 multiply_cosine_fusion
  111.1 1.0 slice_bitcast_fusion.11
  112.1 0.9 slice_bitcast_fusion.30
  132.1 1.9 copy.77
  134.0 9.3 %all-to-all-start.1 = ((f32[32,3,4,256]{3,2,1,0:T(4,128)}), f32[32,3,4,256]{3,2,1,0:T(4,128)}, u32[]{:S(2)}, u32[]{:S(2)}) async-start(f32[32,3,4,256]{3,2,1,0:T(4,128)} %copy.77), calls=%async_computation.1 | async-start | bytes 786432 | tf_op jit(solution)/shard_map/all_to_all | solution.py:157
  143.5 2.6 fusion.99
  146.8 1.7 copy.86
  148.5 1.9 copy.79
  150.4 0.8 copy.85
  151.3 1.9 subtract_convert_fusion
  153.2 1.1 fusion.56
  154.8 1.8 copy.78
  156.6 1.9 reshape.294
  158.5 1.5 convolution_multiply_fusion
  160.0 2.5 multiply_reduce_fusion
  162.7 40.1 %all-gather.4.cloned.1.call-done = bf16[16384,256]{0,1:T(8,128)(2,1)} async-done(((bf16[512,256]{0,1:T(8,128)(2,1)}), bf16[16384,256]{0,1:T(8,128)(2,1)}) %all-gather.4.cloned.1.call-update) | async-done | bytes 8388624 | tf_op jit(solution)/shard_map/all_gather | solution.py:173
  202.9 15.7 %fusion = (f32[2,256]{1,0:T(2,128)S(1)}, f32[16384,256,2]{1,0,2:T(8,128)}) fusion(pred[256,16384]{0,1:T(8,128)(4,1)} %and_or_fusion, bf16[256,2,64]{2,0,1:T(8,128)(2,1)} %get-tuple-element.50, bf16[256,2,64]{2,0,1:T(8,128)(2,1)} %get-tuple-element.49, bf16[16384,256]{0,1:T(8,128)(2,1)} %all-gather.4.cloned.1.call-done), kind=kOutput, calls=%fused_computation.2 | convolution fusion | flops 2172911104 | bytes 42207232 | tf_op jit(solution)/shard_map/qhd,kd->hqk/dot_general | solution.py:184
  218.5 15.7 %fusion.1 = f32[2,256]{1,0:T(2,128)S(1)} fusion(f32[16384,256,2]{1,0,2:T(8,128)} %get-tuple-element.98, f32[2,256]{1,0:T(2,128)S(1)} %broadcast_maximum_fusion, pred[256,16384]{0,1:T(8,128)(4,1)} %and_or_fusion), kind=kLoop, calls=%fused_computation.3 | loop fusion | flops 41942528 | bytes 37752832 | tf_op jit(solution)/shard_map/reduce_sum | solution.py:189
  234.2 17.2 %fusion.27 = bf16[256,2,128]{0,2,1:T(8,128)(2,1)S(1)} fusion(f32[16384,256,2]{1,0,2:T(8,128)} %get-tuple-element.98, f32[2,256]{1,0:T(2,128)S(1)} %broadcast_maximum_fusion, pred[256,16384]{0,1:T(8,128)(4,1)} %and_or_fusion, bf16[16384,256]{0,1:T(8,128)(2,1)} %all-gather.4.cloned.1.call-done, f32[256,2]{0,1:T(2,128)S(1)} %bitcast.367), kind=kOutput, calls=%fused_computation.30 | convolution fusion | flops 2189557760 | bytes 42078208 | tf_op jit(solution)/shard_map/hqk,kd->hqd/dot_general | solution.py:190
  251.4 2.0 fusion.100
  253.5 2.7 convolution_add_fusion
  256.2 0.7 copy.80
  256.9 0.9 add_bitcast_fusion
  257.8 40.0 %reduce-scatter.2.cloned.1.call-done = f32[256,768]{1,0:T(8,128)} async-done(((f32[256,3072]{1,0:T(8,128)}), f32[256,768]{1,0:T(8,128)}) %reduce-scatter.2.cloned.1.call-update) | async-done | bytes 786448 | tf_op jit(solution)/shard_map/reduce_scatter | solution.py:201
  297.8 2.0 fusion.40
  (150 shorter events, 30.9 us)
Async XLA Ops:
  7.2 246.3 %copy-start = (bf16[384,3072]{1,0:T(8,128)(2,1)S(1)}, bf16[384,3072]{1,0:T(8,128)(2,1)}, u32[]{:S(2)}) copy-start(bf16[384,3072]{1,0:T(8,128)(2,1)} %param.34) | copy-start | bytes 7077892
  7.2 35.5 %all-gather.6.cloned.1.call-start = ((), (), s32[]{:S(2)}) async-start(), calls=%async_computation.5 | async-start | bytes 1966080 | tf_op jit(solution)/shard_map/all_gather | solution.py:94
  10.9 46.6 %copy-start.4 = (bf16[1,256,128]{1,2,0:T(8,128)(2,1)}, bf16[1,256,128]{1,2,0:T(8,128)(2,1)S(1)}, u32[]{:S(2)}) copy-start(bf16[1,256,128]{1,2,0:T(8,128)(2,1)S(1)} %copy.66) | copy-start | bytes 196612
  10.9 46.2 %copy-start.21 = (f32[64]{0:T(128)}, f32[64]{0:T(128)S(1)}, u32[]{:S(2)}) copy-start(f32[64]{0:T(128)S(1)} %multiply_power_fusion) | copy-start | bytes 772
  11.5 45.6 %copy-start.16 = (f32[256]{0:T(256)}, f32[256]{0:T(256)S(1)}, u32[]{:S(2)}) copy-start(f32[256]{0:T(256)S(1)} %add_convert_fusion.1) | copy-start | bytes 3076
  42.7 3.9 %copy-start.25 = (bf16[3072,2,384]{2,1,0:T(2,128)(2,1)S(1)}, bf16[3072,2,384]{2,1,0:T(2,128)(2,1)}, u32[]{:S(2)}) copy-start(bf16[3072,2,384]{2,1,0:T(2,128)(2,1)} %param.25) | copy-start | bytes 14155780
  46.6 2.9 copy-start.1
  46.6 2.9 copy-start.8
  46.6 2.9 copy-start.24
  48.1 6.9 %copy-start.3 = (bf16[3072,128]{1,0:T(8,128)(2,1)S(1)}, bf16[3072,128]{1,0:T(8,128)(2,1)}, u32[]{:S(2)}) copy-start(bf16[3072,128]{1,0:T(8,128)(2,1)} %param.23) | copy-start | bytes 2359300
  51.3 7.1 %copy-start.18 = (bf16[3,384]{1,0:T(4,128)(2,1)S(1)}, bf16[3,384]{1,0:T(4,128)(2,1)}, u32[]{:S(2)}) copy-start(bf16[3,384]{1,0:T(4,128)(2,1)} %slice_bitcast_fusion.73) | copy-start | bytes 6916
  51.3 0.8 copy-start.10
  57.1 20.6 %copy-start.12 = (f32[1,512]{1,0:T(1,128)S(1)}, f32[1,512]{1,0:T(1,128)}, u32[]{:S(2)}) copy-start(f32[1,512]{1,0:T(1,128)} %get-tuple-element.90) | copy-start | bytes 6148
  57.1 20.6 %copy-start.13 = (f32[1,512]{1,0:T(1,128)S(1)}, f32[1,512]{1,0:T(1,128)}, u32[]{:S(2)}) copy-start(f32[1,512]{1,0:T(1,128)} %get-tuple-element.91) | copy-start | bytes 6148
  57.1 20.6 %copy-start.14 = (f32[1,512]{1,0:T(1,128)S(1)}, f32[1,512]{1,0:T(1,128)}, u32[]{:S(2)}) copy-start(f32[1,512]{1,0:T(1,128)} %get-tuple-element.92) | copy-start | bytes 6148
  57.1 20.6 %copy-start.15 = (f32[1,512]{1,0:T(1,128)S(1)}, f32[1,512]{1,0:T(1,128)}, u32[]{:S(2)}) copy-start(f32[1,512]{1,0:T(1,128)} %get-tuple-element.93) | copy-start | bytes 6148
  58.2 32.1 %collective-permute-start = (bf16[512,128]{0,1:T(8,128)(2,1)}, bf16[512,128]{0,1:T(8,128)(2,1)}, u32[]{:S(2)}, u32[]{:S(2)}) collective-permute-start(bf16[512,128]{0,1:T(8,128)(2,1)} %pad_maximum_fusion.1), channel_id=1, source_target_pairs={{0,2},{2,0},{4,6},{6,4},{1,3},{3,1},{5,7},{7,5},{8,10},{10,8},{12,... | collective-permute-start | bytes 393224 | tf_op jit(solution)/shard_map/ppermute | solution.py:113
  58.3 15.9 %collective-permute-start.1 = (bf16[3,384]{1,0:T(4,128)(2,1)S(1)}, bf16[3,384]{1,0:T(4,128)(2,1)S(1)}, u32[]{:S(2)}, u32[]{:S(2)}) collective-permute-start(bf16[3,384]{1,0:T(4,128)(2,1)S(1)} %copy-done.18), channel_id=1, source_target_pairs={{0,8},{8,16},{16,24},{24,32},{32,40},{40,48},{48,56},{56,64},{64,7... | collective-permute-start | bytes 6920 | tf_op jit(solution)/shard_map/ppermute | solution.py:19
  71.1 5.7 %collective-permute-start.2 = (bf16[3,512]{1,0:T(4,128)(2,1)S(1)}, bf16[3,512]{1,0:T(4,128)(2,1)S(1)}, u32[]{:S(2)}, u32[]{:S(2)}) collective-permute-start(bf16[3,512]{1,0:T(4,128)(2,1)S(1)} %slice.510), channel_id=1, source_target_pairs={{0,8},{8,16},{16,24},{24,32},{32,40},{40,48},{48,56},{56,64},{64,7... | collective-permute-start | bytes 9224 | tf_op jit(solution)/shard_map/ppermute | solution.py:19
  75.0 4.9 %copy-start.19 = (f32[3]{0:T(128)S(1)}, f32[3]{0:T(128)}, u32[]{:S(2)}) copy-start(f32[3]{0:T(128)} %exp.54) | copy-start | bytes 40
  76.8 13.4 %copy-start.5 = (bf16[1,256,128]{1,2,0:T(8,128)(2,1)S(1)}, bf16[1,256,128]{1,2,0:T(8,128)(2,1)}, u32[]{:S(2)}) copy-start(bf16[1,256,128]{1,2,0:T(8,128)(2,1)} %copy-done.4) | copy-start | bytes 196612
  77.6 14.4 %copy-start.6 = (s32[16384]{0:T(1024)S(1)}, s32[16384]{0:T(1024)}, u32[]{:S(2)}) copy-start(s32[16384]{0:T(1024)} %fusion.80) | copy-start | bytes 196612
  77.7 14.4 %copy-start.7 = (pred[16384]{0:T(1024)(128)(4,1)S(1)}, pred[16384]{0:T(1024)(128)(4,1)}, u32[]{:S(2)}) copy-start(pred[16384]{0:T(1024)(128)(4,1)} %get-tuple-element.104) | copy-start | bytes 49156
  77.7 14.4 %copy-start.22 = (s32[256]{0:T(256)S(1)}, s32[256]{0:T(256)}, u32[]{:S(2)}) copy-start(s32[256]{0:T(256)} %iota_add_fusion) | copy-start | bytes 3076
  79.5 28.2 %copy-start.23 = (bf16[384]{0:T(512)(128)(2,1)S(1)}, bf16[384]{0:T(512)(128)(2,1)}, u32[]{:S(2)}) copy-start(bf16[384]{0:T(512)(128)(2,1)} %param.33) | copy-start | bytes 2308
  80.9 30.1 %all-to-all-start = ((f32[32,3,5,256]{3,1,2,0:T(4,128)}), f32[32,3,5,256]{3,1,2,0:T(4,128)}, u32[]{:S(2)}, u32[]{:S(2)}) async-start(f32[32,3,5,256]{3,1,2,0:T(4,128)} %pad_maximum_fusion), calls=%async_computation | async-start | bytes 1310720 | tf_op jit(solution)/shard_map/all_to_all | solution.py:150
  90.2 112.7 %all-gather.4.cloned.1.call-start = ((), (), s32[]{:S(2)}) async-start(), calls=%async_computation.3 | async-start | bytes 8650752 | tf_op jit(solution)/shard_map/all_gather | solution.py:173
  134.0 20.8 %all-to-all-start.1 = ((f32[32,3,4,256]{3,2,1,0:T(4,128)}), f32[32,3,4,256]{3,2,1,0:T(4,128)}, u32[]{:S(2)}, u32[]{:S(2)}) async-start(f32[32,3,4,256]{3,2,1,0:T(4,128)} %copy.77), calls=%async_computation.1 | async-start | bytes 786432 | tf_op jit(solution)/shard_map/all_to_all | solution.py:157
  143.3 15.2 %copy-start.9 = (f32[256,3]{0,1:T(4,128)S(1)}, f32[256,3]{0,1:T(4,128)}, u32[]{:S(2)}) copy-start(f32[256,3]{0,1:T(4,128)} %get-tuple-element.94) | copy-start | bytes 9220
  143.3 16.7 %copy-start.11 = (f32[1,3,2,128]{3,1,2,0:T(4,128)S(1)}, f32[1,3,2,128]{3,1,2,0:T(4,128)}, u32[]{:S(2)}) copy-start(f32[1,3,2,128]{3,1,2,0:T(4,128)} %copy-done.10) | copy-start | bytes 9220
  143.3 16.7 %copy-start.17 = (f32[256,3]{0,1:T(4,128)S(1)}, f32[256,3]{0,1:T(4,128)}, u32[]{:S(2)}) copy-start(f32[256,3]{0,1:T(4,128)} %get-tuple-element.88) | copy-start | bytes 9220
  143.3 154.5 %reduce-scatter.2.cloned.1.call-start = ((), (), s32[]{:S(2)}) async-start(), calls=%async_computation.4 | async-start | bytes 3932160 | tf_op jit(solution)/shard_map/reduce_scatter | solution.py:201
  253.4 3.5 %copy-start.2 = (f32[3,128,256]{2,1,0:T(8,128)S(1)}, f32[3,128,256]{2,1,0:T(8,128)}, u32[]{:S(2)}) copy-start(f32[3,128,256]{2,1,0:T(8,128)} %reshape.294) | copy-start | bytes 1179652
  253.5 3.5 %copy-start.20 = (f32[3]{0:T(128)S(1)}, f32[3]{0:T(128)}, u32[]{:S(2)}) copy-start(f32[3]{0:T(128)} %exp.54) | copy-start | bytes 40
Sparse Core Ops, SparseCore 0:
  9.8 32.8 all-gather.5
  93.5 109.3 all-gather.3
  256.3 41.4 reduce-scatter.1
where the time goes:
time: 308 us; the launch traced here: 306 us
  waiting for transfers between devices  108 us (35%)
  other arithmetic  75.5 us (25%)
  matrix products  53 us (17%)
  starting transfers between devices  25.2 us (8%)
  local copies, waits for them, and re-layouts  19.5 us (6%)
  between operations  15.1 us (5%)
  blocking collectives  9.69 us (3%)
    all_gather x1, waiting for transfers between devices, shards(): piece = lax.all_gather(group_rows, 'seq', axis=0, tiled=True)  40.1 us
    reduce_scatter x1, waiting for transfers between devices, shards(): summed = lax.psum_scatter(term, 'mp', scatter_dimension=1, tiled=True)  40 us
    all_gather x1, waiting for transfers between devices, shards(): whole = lax.all_gather(own_rows, 'mp', axis=1, tiled=True)  27 us
    unnamed x31, other arithmetic  18.3 us
    dot_general x1, matrix products, shards(): jnp.einsum('hqk,kd->hqd', weights.astype(jnp.bfloat16), piece[:, HD:2 * H...  17.2 us
    reduce_sum x1, other arithmetic, shards(): total = jnp.sum(weights, axis=-1)  15.7 us
    dot_general x1, matrix products, shards(): jnp.einsum('qhd,kd->hqk', query, piece[:, :HD], preferred_element_type=jn...  15.7 us
    or x1, other arithmetic, shards(): slot_ok[None, :]  15.6 us
  transfers between devices with their start and end apart: 8, of which 4 were waited for; matrix products, arithmetic and copies ran while one was open for 25% of the time, Pallas kernels for 0%

commit v1 on v0

--- a/solution.py
+++ b/solution.py
@@ -11,6 +11,18 @@
 epsilon = 1e-05
 rope_base = 100000000000.0
 negative = -1e30
+
+
+def settle_chains_all(unit):
+    return jnp.concatenate(
+        lax.all_to_all(
+            jnp.stack(lax.axis_size("mp") * [unit], axis=0),
+            concat_axis=0,
+            split_axis=0,
+            axis_name="mp",
+        ),
+        axis=1,
+    )
 
 
 def shifted(block, axis, distance):
@@ -91,7 +103,7 @@
     seq_pos = lax.axis_index("seq")
     mp_pos = lax.axis_index("mp")
     length = cache_len[0]
-    whole = lax.all_gather(own_rows, "mp", axis=1, tiled=True)
+    whole = settle_chains_all(own_rows)
     normed = (rms_scale(whole.astype(jnp.float32)) * norm_gain.astype(jnp.float32)).astype(
         jnp.bfloat16
     )

time: 308 us -> 283 us (0.919)
  waiting for transfers between devices: 108 us -> 75.9 us
  starting transfers between devices: 25.2 us -> 33.1 us
  other arithmetic: 75.5 us -> 69.3 us
  local copies, waits for them, and re-layouts: 19.5 us -> 23.2 us
    all_gather x1 -> x0, waiting for transfers between devices: 27 us -> none  [shards(): whole = lax.all_gather(own_rows, 'mp', axis=1, tiled=True)]
    all_gather x1, waiting for transfers between devices: 40.1 us -> 15.1 us  [shards(): piece = lax.all_gather(group_rows, 'seq', axis=0, tiled=True)]
    all_to_all x1, waiting for transfers between devices: 0.49 us -> 11.8 us  [shards(): lax.all_to_all(jnp.stack(entering, axis=0), 'seq', 0, 0, tiled=True)]
    all_to_all x1, waiting for transfers between devices: 0.01 us -> 9.16 us  [shards(): lax.all_to_all(jnp.concatenate([pieces, decays], axis=2), 'seq', 0, 0, ti...]
    all_to_all x0 -> x1, starting transfers between devices: none -> 4.99 us  [settle_chains_all(): lax.all_to_all(jnp.stack(lax.axis_size('mp') * [unit], axis=0), concat_ax...]
  transfers between devices with their start and end apart: 8 -> 8, of which waited for: 4 -> 4; matrix products, arithmetic and copies ran while one was open for 25% -> 26% of each run, Pallas kernels for 0% -> 0%
where the time goes in v1:
time: 283 us; the launch traced here: 282 us
  waiting for transfers between devices  75.9 us (27%)
  other arithmetic  69.3 us (24%)
  matrix products  55.5 us (20%)
  starting transfers between devices  33.1 us (12%)
  local copies, waits for them, and re-layouts  23.2 us (8%)
  between operations  15.3 us (5%)
  blocking collectives  9.65 us (3%)
    reduce_scatter x1, waiting for transfers between devices, shards(): summed = lax.psum_scatter(term, 'mp', scatter_dimension=1, tiled=True)  39.9 us
    unnamed x31, other arithmetic  18.3 us
    dot_general x1, matrix products, shards(): jnp.einsum('hqk,kd->hqd', weights.astype(jnp.bfloat16), piece[:, HD:2 * H...  17.2 us
    reduce_sum x1, other arithmetic, shards(): total = jnp.sum(weights, axis=-1)  15.7 us
    or x1, other arithmetic, shards(): slot_ok[None, :]  15.6 us
    dot_general x1, matrix products, shards(): jnp.einsum('qhd,kd->hqk', query, piece[:, :HD], preferred_element_type=jn...  15.6 us
    all_gather x1, waiting for transfers between devices, shards(): piece = lax.all_gather(group_rows, 'seq', axis=0, tiled=True)  15.1 us
    all_to_all x1, starting transfers between devices, shards(): lax.all_to_all(jnp.concatenate([pieces, decays], axis=2), 'seq', 0, 0, ti...  11.9 us
  transfers between devices with their start and end apart: 8, of which 4 were waited for; matrix products, arithmetic and copies ran while one was open for 26% of the time, Pallas kernels for 0%

profile of v1, /device:TPU:1, one launch (start us, length us, event | category | flops | bytes accessed | tf_op | source)
XLA Modules:
  0.0 282.0 jit_solution(8555985153625332375)
XLA Ops:
  7.2 2.4 stack.100
  9.6 5.0 %all-to-all-start = ((bf16[4,256,768]{2,1,0:T(8,128)(2,1)}), bf16[4,256,768]{2,1,0:T(8,128)(2,1)}, u32[]{:S(2)}, u32[]{:S(2)}) async-start(bf16[4,256,768]{2,1,0:T(8,128)(2,1)} %stack.100), calls=%async_computation | async-start | bytes 3145728 | tf_op jit(solution)/shard_map/all_to_all | solution.py:18
  15.4 15.6 %and_or_fusion = pred[256,16384]{0,1:T(8,128)(4,1)} fusion(s32[256]{0:T(256)S(1)} %iota_add_fusion, s32[16384]{0:T(1024)S(1)} %fusion.78, pred[16384]{0:T(1024)(128)(4,1)S(1)} %get-tuple-element.105, pred[16384]{0:T(1024)(128)(4,1)S(1)} %get-tuple-element.104), kind=kLoop, calls=%fused_computation.7 | loop fusion | flops 12582912 | bytes 4293632 | tf_op jit(solution)/shard_map/or | solution.py:194
  32.3 2.6 copy.108
  35.1 2.6 copy.84
  37.6 1.8 multiply_reduce_fusion
  39.5 1.9 fusion.10
  41.4 1.1 copy-done.1
  42.9 0.9 reduce-window.6
  44.2 2.1 fusion.95
  46.2 4.3 %fusion.12 = bf16[256,2,384]{2,0,1:T(8,128)(2,1)S(1)} fusion(bf16[3072,2,384]{2,1,0:T(2,128)(2,1)} %param.25, bf16[256,3072]{0,1:T(8,128)(2,1)} %copy-done.1), kind=kOutput, calls=%fused_computation.20 | convolution fusion | flops 1208156160 | bytes 6684672 | tf_op jit(solution)/shard_map/td,dkc->tkc/dot_general | solution.py:132
  51.3 1.6 collective-permute-start
  53.0 3.3 %collective-permute-start.1 = (bf16[3,384]{1,0:T(4,128)(2,1)S(1)}, bf16[3,384]{1,0:T(4,128)(2,1)S(1)}, u32[]{:S(2)}, u32[]{:S(2)}) collective-permute-start(bf16[3,384]{1,0:T(4,128)(2,1)S(1)} %slice_bitcast_fusion.73), channel_id=1, source_target_pairs={{0,8},{8,16},{16,24},{24,32},{32,40},{40,48},{48,56},{56,64},{64,7... | collective-permute-start | bytes 6920 | tf_op jit(solution)/shard_map/ppermute | solution.py:31
  56.6 0.8 maximum_select_fusion
  57.9 1.8 slice_convert_fusion
  59.8 2.0 convolution_convert_fusion
  61.8 9.7 %all_gather.7 = bf16[256,512]{1,0:T(8,128)(2,1)S(1)} all-gather(bf16[256,128]{1,0:T(8,128)(2,1)S(1)} %convolution_convert_fusion), channel_id=1, replica_groups=mesh['seq'=32,'mp'=4,'req'=2] {'mp'}, dimensions={1}, use_global_device_ids=true | all-gather | bytes 327680 | tf_op jit(solution)/shard_map/all_gather | solution.py:122
  71.4 3.2 %collective-permute-start.2 = (bf16[3,512]{1,0:T(4,128)(2,1)S(1)}, bf16[3,512]{1,0:T(4,128)(2,1)S(1)}, u32[]{:S(2)}, u32[]{:S(2)}) collective-permute-start(bf16[3,512]{1,0:T(4,128)(2,1)S(1)} %slice.510), channel_id=1, source_target_pairs={{0,8},{8,16},{16,24},{24,32},{32,40},{40,48},{48,56},{56,64},{64,7... | collective-permute-start | bytes 9224 | tf_op jit(solution)/shard_map/ppermute | solution.py:31
  75.0 0.9 copy.92
  76.4 1.5 fusion.43
  78.2 1.0 pad_maximum_fusion
  79.2 11.9 %all-to-all-start.1 = ((f32[32,3,5,256]{3,1,2,0:T(4,128)}), f32[32,3,5,256]{3,1,2,0:T(4,128)}, u32[]{:S(2)}, u32[]{:S(2)}) async-start(f32[32,3,5,256]{3,1,2,0:T(4,128)} %pad_maximum_fusion), calls=%async_computation.1 | async-start | bytes 1310720 | tf_op jit(solution)/shard_map/all_to_all | solution.py:162
  91.1 0.8 constant_dynamic-slice_fusion
  92.5 1.0 multiply_cosine_fusion
  93.5 1.9 copy.99
  95.4 3.1 %multiply_convert_fusion = bf16[4,256,768]{1,2,0:T(8,128)(2,1)} fusion(bf16[4,256,768]{1,2,0:T(8,128)(2,1)} %copy.84, f32[4,768]{1,0:T(4,128)} %mul.664, f32[256]{0:T(256)} %copy-done.9), kind=kLoop, calls=%fused_computation.17 | loop fusion | flops 3145728 | bytes 3159040 | tf_op jit(solution)/shard_map/convert.13
  98.5 9.2 %all-to-all-done.1 = f32[32,3,5,256]{3,1,2,0:T(4,128)} async-done(((f32[32,3,5,256]{3,1,2,0:T(4,128)}), f32[32,3,5,256]{3,1,2,0:T(4,128)}, u32[]{:S(2)}, u32[]{:S(2)}) %all-to-all-start.1) | async-done | bytes 491552 | tf_op jit(solution)/shard_map/all_to_all | solution.py:162
  107.7 1.0 slice_bitcast_fusion.11
  108.7 0.9 slice_bitcast_fusion.30
  128.7 1.9 copy.97
  130.6 7.8 %all-to-all-start.2 = ((f32[32,3,4,256]{3,2,1,0:T(4,128)}), f32[32,3,4,256]{3,2,1,0:T(4,128)}, u32[]{:S(2)}, u32[]{:S(2)}) async-start(f32[32,3,4,256]{3,2,1,0:T(4,128)} %copy.97), calls=%async_computation.2 | async-start | bytes 786432 | tf_op jit(solution)/shard_map/all_to_all | solution.py:169
  138.6 2.6 fusion.96
  141.9 1.1 fusion.54
  143.0 11.8 %all-to-all-done.2 = f32[32,3,4,256]{3,2,1,0:T(4,128)} async-done(((f32[32,3,4,256]{3,2,1,0:T(4,128)}), f32[32,3,4,256]{3,2,1,0:T(4,128)}, u32[]{:S(2)}, u32[]{:S(2)}) %all-to-all-start.2) | async-done | bytes 393248 | tf_op jit(solution)/shard_map/all_to_all | solution.py:169
  154.7 1.8 copy.98
  156.5 1.9 reshape.307
  158.4 1.5 convolution_multiply_fusion
  159.9 2.6 multiply_reduce_fusion.1
  162.5 0.8 fusion.42
  163.3 15.1 %all-gather.2.cloned.1.call-done = bf16[16384,256]{0,1:T(8,128)(2,1)} async-done(((bf16[512,256]{0,1:T(8,128)(2,1)}), bf16[16384,256]{0,1:T(8,128)(2,1)}) %all-gather.2.cloned.1.call-update) | async-done | bytes 8388624 | tf_op jit(solution)/shard_map/all_gather | solution.py:185
  178.4 15.6 %fusion = (f32[2,256]{1,0:T(2,128)S(1)}, f32[16384,256,2]{1,0,2:T(8,128)}) fusion(pred[256,16384]{0,1:T(8,128)(4,1)} %and_or_fusion, bf16[256,2,64]{0,2,1:T(8,128)(2,1)} %get-tuple-element.86, bf16[256,2,64]{0,2,1:T(8,128)(2,1)} %get-tuple-element.85, bf16[16384,256]{0,1:T(8,128)(2,1)} %all-gather.2.cloned.1.call-done), kind=kOutput, calls=%fused_computation.2 | convolution fusion | flops 2172911104 | bytes 42076160 | tf_op jit(solution)/shard_map/qhd,kd->hqk/dot_general | solution.py:196
  194.0 15.7 %fusion.1 = f32[2,256]{1,0:T(2,128)S(1)} fusion(f32[16384,256,2]{1,0,2:T(8,128)} %get-tuple-element.99, f32[2,256]{1,0:T(2,128)S(1)} %broadcast_maximum_fusion, pred[256,16384]{0,1:T(8,128)(4,1)} %and_or_fusion), kind=kLoop, calls=%fused_computation.3 | loop fusion | flops 41942528 | bytes 37752832 | tf_op jit(solution)/shard_map/reduce_sum | solution.py:201
  209.7 17.2 %fusion.26 = bf16[256,2,128]{0,2,1:T(8,128)(2,1)S(1)} fusion(f32[16384,256,2]{1,0,2:T(8,128)} %get-tuple-element.99, f32[2,256]{1,0:T(2,128)S(1)} %broadcast_maximum_fusion, pred[256,16384]{0,1:T(8,128)(4,1)} %and_or_fusion, bf16[16384,256]{0,1:T(8,128)(2,1)} %all-gather.2.cloned.1.call-done, f32[256,2]{0,1:T(2,128)S(1)} %bitcast.379), kind=kOutput, calls=%fused_computation.30 | convolution fusion | flops 2189557760 | bytes 42078208 | tf_op jit(solution)/shard_map/hqk,kd->hqd/dot_general | solution.py:202
  226.9 2.0 fusion.97
  228.9 2.7 convolution_add_fusion
  232.4 0.9 add_bitcast_fusion
  233.3 39.9 %reduce-scatter.2.cloned.1.call-done = f32[256,768]{1,0:T(8,128)} async-done(((f32[256,3072]{1,0:T(8,128)}), f32[256,768]{1,0:T(8,128)}) %reduce-scatter.2.cloned.1.call-update) | async-done | bytes 786448 | tf_op jit(solution)/shard_map/reduce_scatter | solution.py:213
  273.1 2.0 fusion.38
  (145 shorter events, 26.1 us)
Async XLA Ops:
  7.2 221.7 %copy-start = (bf16[384,3072]{1,0:T(8,128)(2,1)S(1)}, bf16[384,3072]{1,0:T(8,128)(2,1)}, u32[]{:S(2)}) copy-start(bf16[384,3072]{1,0:T(8,128)(2,1)} %param.34) | copy-start | bytes 7077892
  9.6 21.4 %copy-start.6 = (bf16[3072]{0:T(1024)(128)(2,1)S(1)}, bf16[3072]{0:T(1024)(128)(2,1)}, u32[]{:S(2)}) copy-start(bf16[3072]{0:T(1024)(128)(2,1)} %param.21) | copy-start | bytes 18436
  9.6 22.0 %copy-start.21 = (f32[3]{0:T(128)S(1)}, f32[3]{0:T(128)}, u32[]{:S(2)}) copy-start(f32[3]{0:T(128)} %param.29) | copy-start | bytes 40
  9.6 22.0 %copy-start.19 = (bf16[384]{0:T(512)(128)(2,1)S(1)}, bf16[384]{0:T(512)(128)(2,1)}, u32[]{:S(2)}) copy-start(bf16[384]{0:T(512)(128)(2,1)} %param.33) | copy-start | bytes 2308
  9.6 22.6 %copy-start.5 = (bf16[1,256,128]{2,1,0:T(8,128)(2,1)S(1)}, bf16[1,256,128]{2,1,0:T(8,128)(2,1)}, u32[]{:S(2)}) copy-start(bf16[1,256,128]{2,1,0:T(8,128)(2,1)} %param.35) | copy-start | bytes 196612
  9.6 25.4 %all-to-all-start = ((bf16[4,256,768]{2,1,0:T(8,128)(2,1)}), bf16[4,256,768]{2,1,0:T(8,128)(2,1)}, u32[]{:S(2)}, u32[]{:S(2)}) async-start(bf16[4,256,768]{2,1,0:T(8,128)(2,1)} %stack.100), calls=%async_computation | async-start | bytes 3145728 | tf_op jit(solution)/shard_map/all_to_all | solution.py:18
  14.6 20.4 %copy-start.8 = (bf16[4,384]{1,0:T(4,128)(2,1)S(1)}, bf16[4,384]{1,0:T(4,128)(2,1)}, u32[]{:S(2)}) copy-start(bf16[4,384]{1,0:T(4,128)(2,1)} %param.31) | copy-start | bytes 9220
  14.6 20.4 %copy-start.7 = (bf16[4,512]{1,0:T(4,128)(2,1)S(1)}, bf16[4,512]{1,0:T(4,128)(2,1)}, u32[]{:S(2)}) copy-start(bf16[4,512]{1,0:T(4,128)(2,1)} %param.32) | copy-start | bytes 12292
  14.6 163.8 %all-gather.2.cloned.1.call-start = ((), (), s32[]{:S(2)}) async-start(), calls=%async_computation.4 | async-start | bytes 8650752 | tf_op jit(solution)/shard_map/all_gather | solution.py:185
  34.9 7.6 %copy-start.20 = (bf16[3072,3]{0,1:T(4,128)(2,1)S(1)}, bf16[3072,3]{0,1:T(4,128)(2,1)}, u32[]{:S(2)}) copy-start(bf16[3072,3]{0,1:T(4,128)(2,1)} %param.27) | copy-start | bytes 55300
  34.9 7.6 %copy-start.22 = (f32[3]{0:T(128)S(1)}, f32[3]{0:T(128)}, u32[]{:S(2)}) copy-start(f32[3]{0:T(128)} %param.28) | copy-start | bytes 40
  34.9 15.6 %copy-start.18 = (f32[64]{0:T(128)}, f32[64]{0:T(128)S(1)}, u32[]{:S(2)}) copy-start(f32[64]{0:T(128)S(1)} %multiply_power_fusion) | copy-start | bytes 772
  35.0 15.6 %copy-start.12 = (f32[256]{0:T(256)}, f32[256]{0:T(256)S(1)}, u32[]{:S(2)}) copy-start(f32[256]{0:T(256)S(1)} %add_convert_fusion.2) | copy-start | bytes 3076
  39.5 4.7 %copy-start.9 = (f32[256]{0:T(256)}, f32[256]{0:T(256)S(1)}, u32[]{:S(2)}) copy-start(f32[256]{0:T(256)S(1)} %add_rsqrt_fusion.1) | copy-start | bytes 3076
  41.4 1.2 copy-start.1
  46.2 13.5 %copy-start.3 = (bf16[3072,128]{1,0:T(8,128)(2,1)S(1)}, bf16[3072,128]{1,0:T(8,128)(2,1)}, u32[]{:S(2)}) copy-start(bf16[3072,128]{1,0:T(8,128)(2,1)} %param.26) | copy-start | bytes 2359300
  50.5 0.7 copy-start.4
  50.6 24.1 %copy-start.15 = (bf16[1,3,384]{2,1,0:T(4,128)(2,1)S(1)}, bf16[1,3,384]{2,1,0:T(4,128)(2,1)}, u32[]{:S(2)}) copy-start(bf16[1,3,384]{2,1,0:T(4,128)(2,1)} %param.37) | copy-start | bytes 6916
  50.9 25.0 %copy-start.13 = (bf16[1,3,512]{2,1,0:T(4,128)(2,1)S(1)}, bf16[1,3,512]{2,1,0:T(4,128)(2,1)}, u32[]{:S(2)}) copy-start(bf16[1,3,512]{2,1,0:T(4,128)(2,1)} %param.38) | copy-start | bytes 9220
  51.3 5.3 %collective-permute-start = (bf16[512,128]{0,1:T(8,128)(2,1)S(1)}, bf16[512,128]{0,1:T(8,128)(2,1)S(1)}, u32[]{:S(2)}, u32[]{:S(2)}) collective-permute-start(bf16[512,128]{0,1:T(8,128)(2,1)S(1)} %pad_maximum_fusion.1), channel_id=1, source_target_pairs={{0,2},{2,0},{4,6},{6,4},{1,3},{3,1},{5,7},{7,5},{8,10},{10,8},{12,... | collective-permute-start | bytes 393224 | tf_op jit(solution)/shard_map/ppermute | solution.py:125
  53.0 23.0 %copy-start.10 = (f32[1,3,2,128]{3,1,2,0:T(4,128)}, f32[1,3,2,128]{3,1,2,0:T(4,128)S(1)}, u32[]{:S(2)}) copy-start(f32[1,3,2,128]{3,1,2,0:T(4,128)S(1)} %copy.133) | copy-start | bytes 9220
  53.0 21.7 %collective-permute-start.1 = (bf16[3,384]{1,0:T(4,128)(2,1)S(1)}, bf16[3,384]{1,0:T(4,128)(2,1)S(1)}, u32[]{:S(2)}, u32[]{:S(2)}) collective-permute-start(bf16[3,384]{1,0:T(4,128)(2,1)S(1)} %slice_bitcast_fusion.73), channel_id=1, source_target_pairs={{0,8},{8,16},{16,24},{24,32},{32,40},{40,48},{48,56},{56,64},{64,7... | collective-permute-start | bytes 6920 | tf_op jit(solution)/shard_map/ppermute | solution.py:31
  71.4 6.7 %copy-start.16 = (f32[3]{0:T(128)}, f32[3]{0:T(128)S(1)}, u32[]{:S(2)}) copy-start(f32[3]{0:T(128)S(1)} %exp.54) | copy-start | bytes 40
  71.4 4.5 %collective-permute-start.2 = (bf16[3,512]{1,0:T(4,128)(2,1)S(1)}, bf16[3,512]{1,0:T(4,128)(2,1)S(1)}, u32[]{:S(2)}, u32[]{:S(2)}) collective-permute-start(bf16[3,512]{1,0:T(4,128)(2,1)S(1)} %slice.510), channel_id=1, source_target_pairs={{0,8},{8,16},{16,24},{24,32},{32,40},{40,48},{48,56},{56,64},{64,7... | collective-permute-start | bytes 9224 | tf_op jit(solution)/shard_map/ppermute | solution.py:31
  79.2 28.4 %all-to-all-start.1 = ((f32[32,3,5,256]{3,1,2,0:T(4,128)}), f32[32,3,5,256]{3,1,2,0:T(4,128)}, u32[]{:S(2)}, u32[]{:S(2)}) async-start(f32[32,3,5,256]{3,1,2,0:T(4,128)} %pad_maximum_fusion), calls=%async_computation.1 | async-start | bytes 1310720 | tf_op jit(solution)/shard_map/all_to_all | solution.py:162
  130.5 29.3 %copy-start.11 = (f32[1,3,2,128]{3,1,2,0:T(4,128)S(1)}, f32[1,3,2,128]{3,1,2,0:T(4,128)}, u32[]{:S(2)}) copy-start(f32[1,3,2,128]{3,1,2,0:T(4,128)} %copy-done.10) | copy-start | bytes 9220
  130.5 29.4 %copy-start.14 = (f32[256,3]{0,1:T(4,128)S(1)}, f32[256,3]{0,1:T(4,128)}, u32[]{:S(2)}) copy-start(f32[256,3]{0,1:T(4,128)} %get-tuple-element.89) | copy-start | bytes 9220
  130.6 24.2 %all-to-all-start.2 = ((f32[32,3,4,256]{3,2,1,0:T(4,128)}), f32[32,3,4,256]{3,2,1,0:T(4,128)}, u32[]{:S(2)}, u32[]{:S(2)}) async-start(f32[32,3,4,256]{3,2,1,0:T(4,128)} %copy.97), calls=%async_computation.2 | async-start | bytes 786432 | tf_op jit(solution)/shard_map/all_to_all | solution.py:169
  138.3 134.8 %reduce-scatter.2.cloned.1.call-start = ((), (), s32[]{:S(2)}) async-start(), calls=%async_computation.5 | async-start | bytes 3932160 | tf_op jit(solution)/shard_map/reduce_scatter | solution.py:213
  228.9 3.5 %copy-start.2 = (f32[3,128,256]{2,1,0:T(8,128)S(1)}, f32[3,128,256]{2,1,0:T(8,128)}, u32[]{:S(2)}) copy-start(f32[3,128,256]{2,1,0:T(8,128)} %reshape.307) | copy-start | bytes 1179652
  228.9 3.5 %copy-start.17 = (f32[3]{0:T(128)S(1)}, f32[3]{0:T(128)}, u32[]{:S(2)}) copy-start(f32[3]{0:T(128)} %copy-done.16) | copy-start | bytes 40
Sparse Core Ops, SparseCore 0:
  57.5 120.8 all-gather.1
  231.8 41.3 reduce-scatter.1
